TPU v7x, 512 devices: a whole 4x8x8 slice. The times are simulated.
512 devices in a mesh: req: 32 (over y_hi, x, core), tp: 16 (over z, y_lo).
Axes of the slice: x: 4, y: 8 (y_hi: 4, y_lo: 2; y = y_hi * 2 + y_lo), z: 8, core: 2. Of those that a mesh axis runs over, the one named last changes fastest.
Arguments:
- hidden: bfloat16 [32, 256, 4096], P('req', None, 'tp'), may hold values from -6 to 6
- norm_gain: bfloat16 [4096], P('tp'), may hold values from 0.5 to 1.5
- w_query: bfloat16 [4096, 2048], P(None, 'tp'), may hold values from -0.09375 to 0.09375
- w_key: bfloat16 [4096, 2048], P(None, 'tp'), may hold values from -0.09375 to 0.09375
- w_value: bfloat16 [4096, 2048], P(None, 'tp'), may hold values from -0.09375 to 0.09375
- w_out: bfloat16 [2048, 4096], P('tp'), may hold values from -0.5 to 0.5
- prefix_keys: bfloat16 [16384, 2048], P('req', 'tp'), may hold values from -1000 to 1000
- prefix_values: bfloat16 [16384, 2048], P('req', 'tp'), may hold values from -6 to 6
- lengths: int32 [32], P('req'), may hold values from 32 to 256, as said below
Outputs:
- attended: bfloat16 [32, 256, 4096], P('req', 'tp')
Inputs may be any that keep to these rules, and one draw needn't show every extreme that they name: `lengths`: every request has at least 32 suffix tokens; in every draw some request has exactly 256.
All inputs are finite; a program needn't handle non-finite values.
Results may differ from a plain program's by a relative error of at most 0.029.
Values may be sent and summed in bfloat16 or wider, within the bound.
A program may use at most 64 MiB of HBM per device.

v0:
```python
import jax
import jax.numpy as jnp
from jax import lax
from jax.sharding import PartitionSpec as P


def rotate(values, angles):
    half = values.shape[-1] // 2
    cosine = jnp.cos(angles)
    sine = jnp.sin(angles)
    first = values[..., :half]
    second = values[..., half:]
    return jnp.concatenate(
        [first * cosine - second * sine, second * cosine + first * sine], axis=-1
    )


def on_device(
    hidden, norm_gain, w_query, w_key, w_value, w_out, prefix_keys, prefix_values, lengths
):
    full, gain = (
        lax.all_gather(hidden, "tp", axis=2, tiled=True),
        lax.all_gather(norm_gain, "tp", axis=0, tiled=True),
    )
    x = full[0].astype(jnp.float32)
    slot = x.shape[0]
    head_dim = w_query.shape[1]
    groups = lax.axis_size("req")
    prefix = prefix_keys.shape[0] * groups
    normed = (
        x * lax.rsqrt(jnp.mean(x * x, axis=-1, keepdims=True) + 1e-05) * gain.astype(jnp.float32)
    ).astype(jnp.bfloat16)
    positions = (prefix + jnp.arange(slot)).astype(jnp.float32)
    freq = 10000.0 ** (-2.0 * jnp.arange(head_dim // 2).astype(jnp.float32) / head_dim)
    angles = positions[:, None] * freq[None, :]
    query = rotate(jnp.dot(normed, w_query, preferred_element_type=jnp.float32), angles).astype(
        jnp.bfloat16
    )
    key_new = rotate(jnp.dot(normed, w_key, preferred_element_type=jnp.float32), angles).astype(
        jnp.bfloat16
    )
    value_new = jnp.dot(normed, w_value, preferred_element_type=jnp.float32).astype(jnp.bfloat16)
    scale = 1.0 / head_dim**0.5
    causal = jnp.arange(slot)[:, None] >= jnp.arange(slot)[None, :]
    own_scores = jnp.einsum("sd,td->st", query, key_new, preferred_element_type=jnp.float32) * scale
    own_scores = jnp.where(causal, own_scores, -jnp.inf)
    top = jnp.max(own_scores, axis=-1)
    own_weights = jnp.where(causal, jnp.exp(own_scores - top[:, None]), 0.0).astype(jnp.bfloat16)
    total = jnp.sum(own_weights.astype(jnp.float32), axis=-1)
    acc = jnp.dot(own_weights, value_new, preferred_element_type=jnp.float32)
    run_total = total
    run_acc = acc
    keys = lax.all_gather(prefix_keys, "req", axis=0, tiled=True)
    values = lax.all_gather(prefix_values, "req", axis=0, tiled=True)
    scores = jnp.einsum("sd,pd->sp", query, keys, preferred_element_type=jnp.float32) * scale
    new_top = jnp.maximum(top, jnp.max(scores, axis=-1))
    fade = jnp.exp(top - new_top)
    weights = jnp.exp(scores - new_top[:, None]).astype(jnp.bfloat16)
    run_total = run_total * fade + jnp.sum(weights.astype(jnp.float32), axis=-1)
    run_acc = run_acc * fade[:, None] + jnp.dot(weights, values, preferred_element_type=jnp.float32)
    context = (run_acc / run_total[:, None]).astype(jnp.bfloat16)
    rows = slot // lax.axis_size("tp")
    summed = lax.psum_scatter(
        jnp.dot(context, w_out, preferred_element_type=jnp.float32).astype(jnp.bfloat16),
        "tp",
        scatter_dimension=0,
        tiled=True,
    ).astype(jnp.float32)
    index = lax.axis_index("tp") * rows + jnp.arange(rows)
    keep = index < lengths[0]
    return jnp.where(keep[:, None], summed, 0.0).astype(jnp.bfloat16)[None]


def solution(mesh):
    return jax.shard_map(
        on_device,
        mesh=mesh,
        in_specs=(
            P("req", None, "tp"),
            P("tp"),
            P(None, "tp"),
            P(None, "tp"),
            P(None, "tp"),
            P("tp", None),
            P("req", "tp"),
            P("req", "tp"),
            P("req"),
        ),
        out_specs=P("req", "tp", None),
        check_vma=False,
    )
```

profile of v0, /device:TPU:16, one launch (start us, length us, event | category | flops | bytes accessed | tf_op | source)
XLA Modules:
  0.0 325.2 jit_solution(8467891159178002061)
XLA Ops:
  6.5 0.7 all-gather.5.cloned.1.call-update
  7.3 0.0 all-gather.7.cloned.1.call-start
  7.3 0.7 all-gather.7.cloned.1.call-update
  8.0 0.0 all-gather.9.cloned.1.call-start
  8.1 0.7 all-gather.9.cloned.1.call-update
  8.7 0.0 reduce-scatter.2.cloned.1.call-start
  8.8 0.7 reshape.50
  9.5 39.7 %all-gather = bf16[16,1,256]{2,1,0:T(2,128)(2,1)S(1)} all-gather(bf16[1,1,256]{2,1,0:T(2,128)(2,1)S(1)} %reshape.50), channel_id=1, replica_groups=mesh['req'=32,'tp'=16] {'tp'}, dimensions={0}, use_global_device_ids=true | all-gather | bytes 8704 | tf_op jit(solution)/shard_map/all_gather | solution.py:23
  49.2 44.2 %all-gather.5.cloned.1.call-done = bf16[1,256,4096]{2,1,0:T(8,128)(2,1)} async-done(((bf16[1,256,256]{2,1,0:T(8,128)(2,1)}), bf16[1,256,4096]{2,1,0:T(8,128)(2,1)}) %all-gather.5.cloned.1.call-update) | async-done | bytes 2097168 | tf_op jit(solution)/shard_map/all_gather | solution.py:22
  93.4 2.2 fusion
  95.7 2.9 fusion.34
  98.6 1.0 fusion.36
  99.6 0.3 fusion.21
  99.9 0.2 fusion.38
  100.2 0.1 convert_reduce_fusion.1
  100.2 0.9 convolution_convert_fusion.1
  101.1 58.9 %all-gather.7.cloned.1.call-done = bf16[16384,128]{1,0:T(8,128)(2,1)} async-done(((bf16[512,128]{1,0:T(8,128)(2,1)}), bf16[16384,128]{1,0:T(8,128)(2,1)}) %all-gather.7.cloned.1.call-update) | async-done | bytes 4194320 | tf_op jit(solution)/shard_map/all_gather | solution.py:53
  160.0 4.6 %fusion.39 = (f32[256]{0:T(256)S(1)}, f32[256,16384]{1,0:T(8,128)S(1)}) fusion(bf16[16384,128]{1,0:T(8,128)(2,1)} %all-gather.7.cloned.1.call-done, bf16[256,64]{0,1:T(8,128)(2,1)S(1)} %get-tuple-element.13, bf16[256,64]{0,1:T(8,128)(2,1)S(1)} %get-tuple-element.14), kind=kOutput, calls=%fused_computation.57 | convolution fusion | flops 1082261248 | bytes 21038080 | tf_op jit(solution)/shard_map/sd,pd->sp/dot_general | solution.py:55
  164.7 5.4 %convert_reduce_fusion = (f32[256]{0:T(256)S(1)}, bf16[256,16384]{1,0:T(8,128)(2,1)}) fusion(f32[256,16384]{1,0:T(8,128)S(1)} %get-tuple-element.18, f32[256]{0:T(256)S(1)} %max.13), kind=kLoop, calls=%fused_computation.1 | loop fusion | flops 16776960 | bytes 25167872 | tf_op jit(solution)/shard_map/reduce_sum | solution.py:59
  170.1 56.6 %all-gather.9.cloned.1.call-done = bf16[16384,128]{1,0:T(8,128)(2,1)} async-done(((bf16[512,128]{1,0:T(8,128)(2,1)}), bf16[16384,128]{1,0:T(8,128)(2,1)}) %all-gather.9.cloned.1.call-update) | async-done | bytes 4194320 | tf_op jit(solution)/shard_map/all_gather | solution.py:54
  226.7 6.9 %fusion.40 = f32[256,128]{1,0:T(8,128)S(1)} fusion(bf16[256,16384]{1,0:T(8,128)(2,1)} %get-tuple-element.8, bf16[16384,128]{1,0:T(8,128)(2,1)} %all-gather.9.cloned.1.call-done), kind=kOutput, calls=%fused_computation.58 | convolution fusion | flops 1073741824 | bytes 12713984 | tf_op jit(solution)/shard_map/dot_general | solution.py:60
  233.6 2.2 convolution_convert_fusion
  236.5 80.5 %reduce-scatter.2.cloned.1.call-done = bf16[16,4096]{1,0:T(8,128)(2,1)} async-done(((bf16[256,4096]{1,0:T(8,128)(2,1)}), bf16[16,4096]{1,0:T(8,128)(2,1)}) %reduce-scatter.2.cloned.1.call-update) | async-done | bytes 131088 | tf_op jit(solution)/shard_map/reduce_scatter | solution.py:63
  317.0 1.6 fusion.7
  (17 shorter events, 0.1 us)
Async XLA Ops:
  6.5 227.1 %copy-start = (bf16[128,4096]{1,0:T(8,128)(2,1)S(1)}, bf16[128,4096]{1,0:T(8,128)(2,1)}, u32[]{:S(2)}) copy-start(bf16[128,4096]{1,0:T(8,128)(2,1)} %param.14) | copy-start | bytes 3145732
  6.5 92.1 %copy-start.2 = (bf16[4096,128]{1,0:T(8,128)(2,1)S(1)}, bf16[4096,128]{1,0:T(8,128)(2,1)}, u32[]{:S(2)}) copy-start(bf16[4096,128]{1,0:T(8,128)(2,1)} %param.11) | copy-start | bytes 3145732
  6.5 86.9 %all-gather.5.cloned.1.call-start = ((), (), s32[]{:S(2)}) async-start(), calls=%async_computation.1 | async-start | bytes 2228224 | tf_op jit(solution)/shard_map/all_gather | solution.py:22
  7.3 152.8 %all-gather.7.cloned.1.call-start = ((), (), s32[]{:S(2)}) async-start(), calls=%async_computation.2 | async-start | bytes 4325376 | tf_op jit(solution)/shard_map/all_gather | solution.py:53
  8.0 218.7 %all-gather.9.cloned.1.call-start = ((), (), s32[]{:S(2)}) async-start(), calls=%async_computation.3 | async-start | bytes 4325376 | tf_op jit(solution)/shard_map/all_gather | solution.py:54
  8.7 308.3 %reduce-scatter.2.cloned.1.call-start = ((), (), s32[]{:S(2)}) async-start(), calls=%async_computation.4 | async-start | bytes 2228224 | tf_op jit(solution)/shard_map/reduce_scatter | solution.py:63
  93.4 5.2 %copy-start.1 = (bf16[1,256,4096]{2,1,0:T(8,128)(2,1)S(1)}, bf16[1,256,4096]{2,1,0:T(8,128)(2,1)}, u32[]{:S(2)}) copy-start(bf16[1,256,4096]{2,1,0:T(8,128)(2,1)} %all-gather.5.cloned.1.call-done) | copy-start | bytes 6291460
  95.7 4.6 %copy-start.3 = (bf16[4096,128]{1,0:T(8,128)(2,1)S(1)}, bf16[4096,128]{1,0:T(8,128)(2,1)}, u32[]{:S(2)}) copy-start(bf16[4096,128]{1,0:T(8,128)(2,1)} %param.13) | copy-start | bytes 3145732
Sparse Core Ops, SparseCore 0:
  9.3 84.0 all-gather.4
  96.6 63.4 all-gather.6
  163.2 63.4 all-gather.8
  236.0 80.9 reduce-scatter.1
where the time goes:
time: 326 us; the launch traced here: 325 us
  waiting for transfers between devices  242 us (74%)
  blocking collectives  39.7 us (12%)
  matrix products  18.7 us (6%)
  between operations  13.9 us (4%)
  other arithmetic  9.72 us (3%)
    reduce_scatter x1, waiting for transfers between devices, on_device(): lax.psum_scatter(jnp.dot(context, w_out, preferred_element_type=jnp.float...  80.5 us
    all_gather x1, waiting for transfers between devices, on_device(): keys = lax.all_gather(prefix_keys, 'req', axis=0, tiled=True)  58.9 us
    all_gather x1, waiting for transfers between devices, on_device(): values = lax.all_gather(prefix_values, 'req', axis=0, tiled=True)  56.6 us
    all_gather x1, waiting for transfers between devices, on_device(): lax.all_gather(hidden, 'tp', axis=2, tiled=True)  44.2 us
    all_gather x1, blocking collectives, on_device(): lax.all_gather(norm_gain, 'tp', axis=0, tiled=True)  39.7 us
    dot_general x1, matrix products, on_device(): jnp.dot(weights, values, preferred_element_type=jnp.float32)  6.9 us
  transfers between devices with their start and end apart: 4, of which 4 were waited for; matrix products, arithmetic and copies ran while one was open for 6% of the time, Pallas kernels for 0%

commit v1 on v0

v1 whole, which is shorter than its diff:
```python
import jax
import jax.numpy as jnp
from jax import lax
from jax.experimental import pallas as pl
from jax.experimental.pallas import tpu as pltpu
from jax.sharding import PartitionSpec as P

NX = 4
NY = 4
NZ = 8
MESH = pl.DeviceIdType.MESH


def where_am_i():
    r = lax.axis_index("req")
    t = lax.axis_index("tp")
    core = lax.rem(r, 2)
    x = lax.rem(lax.div(r, 2), NX)
    y = lax.div(r, 2 * NX)
    z = lax.div(t, 2)
    low = lax.rem(t, 2)
    return r, t, core, x, y, z, low


def neighbours():
    r, t, core, x, y, z, low = where_am_i()

    def req(yy, xx, cc):
        return (yy * NX + xx) * 2 + cc

    return dict(
        xp=(req(y, lax.rem(x + 1, NX), core), t),
        xm=(req(y, lax.rem(x + NX - 1, NX), core), t),
        yp=(req(lax.rem(y + 1, NY), x, core), t),
        ym=(req(lax.rem(y + NY - 1, NY), x, core), t),
        sib=(req(y, x, 1 - core), t),
        zp=(r, lax.rem(z + 1, NZ) * 2 + low),
        zm=(r, lax.rem(z + NZ - 1, NZ) * 2 + low),
        peer=(r, z * 2 + 1 - low),
    )


def greet(ids):
    barrier = pltpu.get_barrier_semaphore()
    for dev in ids:
        pl.semaphore_signal(barrier, inc=1, device_id=dev, device_id_type=MESH)
    pl.semaphore_wait(barrier, len(ids))


def remote(src, dst, send_sem, recv_sem, dev):
    return pltpu.make_async_remote_copy(
        src_ref=src, dst_ref=dst, send_sem=send_sem, recv_sem=recv_sem,
        device_id=dev, device_id_type=MESH,
    )


def gather_kernel(
    h_ref, k_ref, v_ref, hid, keys, vals, peer_s, peer_r, z_s, z_r, ring_s, ring_r, sib_s, sib_r, own_sem
):
    _, _, _, _, _, z, low = where_am_i()
    n = neighbours()
    greet(list(n.values()))
    own = (k_ref, v_ref)
    full = (keys, vals)
    sends = []

    def start(copy):
        copy.start()
        sends.append(copy)

    def block(a, dy, dx):
        return own[a] if dy == 0 and dx == 0 else full[a].at[0, dy, dx]

    def ring_copy(a, src, slot, dev):
        dy, dx = slot
        return remote(src, full[a].at[0, dy, dx], ring_s.at[a, dy, dx], ring_r.at[a, dy, dx], dev)

    def to_y(a, dy, forward):
        slot = ((dy + (NY - 1 if forward else 1)) % NY, 0)
        start(ring_copy(a, block(a, dy, 0), slot, n["yp"] if forward else n["ym"]))

    def to_x(a, dy, dx, forward):
        slot = (dy, (dx + (NX - 1 if forward else 1)) % NX)
        start(ring_copy(a, block(a, dy, dx), slot, n["xp"] if forward else n["xm"]))

    def sib_copy(a, dy, dx):
        return remote(
            block(a, dy, dx), full[a].at[1, dy, dx], sib_s.at[a, dy, dx], sib_r.at[a, dy, dx], n["sib"]
        )

    def to_sib(a, dy, dx):
        start(sib_copy(a, dy, dx))

    def arrived(a, dy, dx):
        ring_copy(a, full[a].at[0, dy, dx], (dy, dx), n["xp"]).wait_recv()

    def shard(dist, unit):
        zz = lax.rem(z + dist + NZ, NZ)
        return hid.at[zz * 2 + (low if unit == 0 else 1 - low)]

    def z_copy(way, step, unit):
        dist = -(step - 1) if way == 0 else step - 1
        src = h_ref if step == 1 and unit == 0 else shard(dist, unit)
        return remote(
            src, shard(dist, unit), z_s.at[way, step - 1, unit], z_r.at[way, step - 1, unit],
            n["zp"] if way == 0 else n["zm"],
        )

    def z_arrived(way, step, unit):
        dist = -step if way == 0 else step
        buf = shard(dist, unit)
        remote(buf, buf, z_s.at[way, step - 1, unit], z_r.at[way, step - 1, unit], n["zp"]).wait_recv()

    def z_step(step):
        for unit in (0, 1):
            for way in (0, 1):
                if step == NZ // 2 and unit != way:
                    continue
                z_arrived(way, step, unit)
                if step + 1 < NZ // 2 or (step + 1 == NZ // 2 and unit == way):
                    start(z_copy(way, step + 1, unit))

    def x_first(dy):
        for a, dx, forward in ((0, NX - 1, True), (1, 1, False), (1, NX - 1, None), (0, 1, None)):
            arrived(a, dy, dx)
            if forward is not None:
                to_x(a, dy, dx, forward)
            to_sib(a, dy, dx)

    def x_second(dy):
        for a in (0, 1):
            arrived(a, dy, 2)
            to_sib(a, dy, 2)

    def y_done(a, dy):
        to_x(a, dy, 0, True)
        to_x(a, dy, 0, False)
        to_sib(a, dy, 0)

    peer = remote(h_ref, hid.at[z * 2 + low], peer_s, peer_r, n["peer"])
    start(peer)
    for way in (0, 1):
        start(z_copy(way, 1, 0))
    for a in (0, 1):
        to_y(a, 0, True)
        to_y(a, 0, False)
        to_x(a, 0, 0, True)
        to_x(a, 0, 0, False)
    locals_ = [
        pltpu.make_async_copy(h_ref, hid.at[z * 2 + low], own_sem.at[0]),
        pltpu.make_async_copy(k_ref, keys.at[0, 0, 0], own_sem.at[1]),
        pltpu.make_async_copy(v_ref, vals.at[0, 0, 0], own_sem.at[2]),
    ]
    for c in locals_:
        c.start()
    for a in (0, 1):
        to_sib(a, 0, 0)

    theirs = hid.at[z * 2 + 1 - low]
    remote(theirs, theirs, peer_s, peer_r, n["peer"]).wait_recv()
    for way in (0, 1):
        start(z_copy(way, 1, 1))
    x_first(0)
    z_step(1)
    for a, dy, forward in ((0, NY - 1, True), (1, 1, False), (1, NY - 1, None), (0, 1, None)):
        arrived(a, dy, 0)
        if forward is not None:
            to_y(a, dy, forward)
        y_done(a, dy)
    z_step(2)
    x_second(0)
    x_first(3)
    z_step(3)
    for a in (0, 1):
        arrived(a, 2, 0)
        y_done(a, 2)
    x_first(1)
    z_step(4)
    x_second(3)
    x_second(1)
    x_first(2)
    x_second(2)
    for a in (0, 1):
        for dy in range(NY):
            for dx in range(NX):
                sib_copy(a, dy, dx).wait_recv()
    for c in locals_:
        c.wait()
    for c in sends:
        c.wait_send()


def gather(hidden, prefix_keys, prefix_values):
    rows, width = prefix_keys.shape
    slots = jax.ShapeDtypeStruct((2, NY, NX, rows, width), prefix_keys.dtype)
    dma = pltpu.SemaphoreType.DMA
    return pl.pallas_call(
        gather_kernel,
        out_shape=(jax.ShapeDtypeStruct((NZ * 2, *hidden.shape), hidden.dtype), slots, slots),
        in_specs=[pl.BlockSpec(memory_space=pltpu.VMEM)] * 3,
        out_specs=(pl.BlockSpec(memory_space=pl.ANY),) * 3,
        scratch_shapes=[
            dma, dma, dma((2, NZ // 2, 2)), dma((2, NZ // 2, 2)),
            dma((2, NY, NX)), dma((2, NY, NX)), dma((2, NY, NX)), dma((2, NY, NX)), dma((3,)),
        ],
        compiler_params=pltpu.CompilerParams(collective_id=0, has_side_effects=True),
        name="gather_all",
    )(hidden, prefix_keys, prefix_values)


def reduce_rows(terms):
    return lax.psum_scatter(terms, "tp", scatter_dimension=0, tiled=True).astype(jnp.float32)


def rotate(values, angles):
    half = values.shape[-1] // 2
    cosine = jnp.cos(angles)
    sine = jnp.sin(angles)
    first = values[..., :half]
    second = values[..., half:]
    return jnp.concatenate(
        [first * cosine - second * sine, second * cosine + first * sine], axis=-1
    )


def on_device(
    hidden, norm_gain, w_query, w_key, w_value, w_out, prefix_keys, prefix_values, lengths
):
    slot, part = hidden.shape[1:]
    shard = jnp.concatenate([hidden[0], jnp.broadcast_to(norm_gain[None], (16, part))])
    hid, keys, values = gather(shard, prefix_keys, prefix_values)
    blocks = hid.shape[0]
    head_dim = w_query.shape[1]
    keys = keys.reshape(-1, head_dim)
    values = values.reshape(-1, head_dim)
    prefix = keys.shape[0]
    x = hid[:, :slot].astype(jnp.float32)
    gain = hid[:, slot : slot + 1].astype(jnp.float32)
    normed = (
        x * lax.rsqrt(jnp.mean(x * x, axis=(0, 2), keepdims=True) + 1e-05) * gain
    ).astype(jnp.bfloat16)

    def project(w):
        return jnp.einsum(
            "tsf,tfd->sd", normed, w.reshape(blocks, part, head_dim), preferred_element_type=jnp.float32
        )

    positions = (prefix + jnp.arange(slot)).astype(jnp.float32)
    freq = 10000.0 ** (-2.0 * jnp.arange(head_dim // 2).astype(jnp.float32) / head_dim)
    angles = positions[:, None] * freq[None, :]
    query = rotate(project(w_query), angles).astype(jnp.bfloat16)
    key_new = rotate(project(w_key), angles).astype(jnp.bfloat16)
    value_new = project(w_value).astype(jnp.bfloat16)
    scale = 1.0 / head_dim**0.5
    causal = jnp.arange(slot)[:, None] >= jnp.arange(slot)[None, :]
    own_scores = jnp.einsum("sd,td->st", query, key_new, preferred_element_type=jnp.float32) * scale
    own_scores = jnp.where(causal, own_scores, -jnp.inf)
    top = jnp.max(own_scores, axis=-1)
    own_weights = jnp.where(causal, jnp.exp(own_scores - top[:, None]), 0.0).astype(jnp.bfloat16)
    total = jnp.sum(own_weights.astype(jnp.float32), axis=-1)
    acc = jnp.dot(own_weights, value_new, preferred_element_type=jnp.float32)
    scores = jnp.einsum("sd,pd->sp", query, keys, preferred_element_type=jnp.float32) * scale
    new_top = jnp.maximum(top, jnp.max(scores, axis=-1))
    fade = jnp.exp(top - new_top)
    weights = jnp.exp(scores - new_top[:, None]).astype(jnp.bfloat16)
    run_total = total * fade + jnp.sum(weights.astype(jnp.float32), axis=-1)
    run_acc = acc * fade[:, None] + jnp.dot(weights, values, preferred_element_type=jnp.float32)
    context = (run_acc / run_total[:, None]).astype(jnp.bfloat16)
    rows = slot // lax.axis_size("tp")
    terms = jnp.dot(context, w_out, preferred_element_type=jnp.float32).astype(jnp.bfloat16)
    summed = reduce_rows(terms)
    index = lax.axis_index("tp") * rows + jnp.arange(rows)
    keep = index < lengths[0]
    return jnp.where(keep[:, None], summed, jnp.zeros_like(summed)).astype(jnp.bfloat16)[None]


def solution(mesh):
    return jax.shard_map(
        on_device,
        mesh=mesh,
        in_specs=(
            P("req", None, "tp"),
            P("tp"),
            P(None, "tp"),
            P(None, "tp"),
            P(None, "tp"),
            P("tp", None),
            P("req", "tp"),
            P("req", "tp"),
            P("req"),
        ),
        out_specs=P("req", "tp", None),
        check_vma=False,
    )
```

time: 326 us -> 179 us (0.55)
  the two profiles are of different devices: /device:TPU:16 before, /device:TPU:2 now
where the time goes in v1:
time: 179 us
  waiting for transfers between devices  78.7 us (44%)
  Pallas kernels  59.8 us (33%)
  between operations  14.2 us (8%)
  other arithmetic  12.6 us (7%)
  matrix products  12.5 us (7%)
    reduce_scatter x1, waiting for transfers between devices, reduce_rows(): lax.psum_scatter(terms, 'tp', scatter_dimension=0, tiled=True)  78.6 us
    pallas_call x1, Pallas kernels, gather(): pl.pallas_call(gather_kernel, out_shape=(jax.ShapeDtypeStruct((NZ * 2, *h...  59.8 us
    reduce_sum x1, other arithmetic, on_device(): run_total = total * fade + jnp.sum(weights.astype(jnp.float32), axis=-1)  3.69 us
  transfers between devices with their start and end apart: 1, of which 1 were waited for; matrix products, arithmetic and copies ran while one was open for 0% of the time, Pallas kernels for 0%

profile of v1, /device:TPU:2, one launch (start us, length us, event | category | flops | bytes accessed | tf_op | source)
XLA Modules:
  0.0 178.7 jit_solution(10860066237719805361)
XLA Ops:
  6.5 0.0 copy-start
  6.5 0.0 reduce-scatter.2.cloned.1.call-start
  6.5 0.7 broadcast_in_dim.19
  7.3 1.6 pad_maximum_fusion.h_ref
  8.8 59.8 %gather_all.1 = (bf16[16,272,256]{2,1,0:T(8,128)(2,1)}, bf16[2,4,4,512,128]{4,3,2,1,0:T(8,128)(2,1)}, bf16[2,4,4,512,128]{4,3,2,1,0:T(8,128)(2,1)}) custom-call(bf16[272,256]{1,0:T(8,128)(2,1)} %pad_maximum_fusion.h_ref, bf16[512,128]{1,0:T(8,128)(2,1)} %k_ref.1, bf16[512,128]{1,0:T(8,128)(2,1)} %v_ref.1), custom_call_target="tpu_custom_call" | custom-call | tf_op jit(solution)/shard_map/gather_all/pallas_call | solution.py:197
  68.6 0.0 copy-start.3
  68.6 0.9 slice_convert_fusion
  69.6 2.1 %fusion = f32[256]{0:T(256)S(1)} fusion(bf16[16,272,256]{2,1,0:T(8,128)(2,1)} %get-tuple-element.8), kind=kLoop, calls=%fused_computation.6 | loop fusion | flops 3145472 | bytes 2098176 | tf_op jit(solution)/shard_map/reduce_sum | solution.py:240
  71.7 2.3 %fusion.2 = bf16[16,256,256]{2,1,0:T(8,128)(2,1)S(1)} fusion(f32[16,256]{1,0:T(8,128)S(1)} %bitcast.39, f32[256]{0:T(256)S(1)} %add_rsqrt_fusion, bf16[16,272,256]{2,1,0:T(8,128)(2,1)} %get-tuple-element.8), kind=kLoop, calls=%fused_computation.8 | loop fusion | flops 4194304 | bytes 4211712 | tf_op jit(solution)/shard_map/convert_element_type | solution.py:241
  74.0 0.8 convolution_bitcast_fusion.1
  74.9 0.0 copy-done.4
  74.9 0.8 convolution_bitcast_fusion.2
  75.7 0.3 fusion.22
  76.1 0.1 copy-done.2
  76.2 2.5 %fusion.32 = (f32[256]{0:T(256)S(1)}, f32[256,16384]{1,0:T(8,128)S(1)}) fusion(bf16[16384,128]{1,0:T(8,128)(2,1)S(1)} %bitcast.35, bf16[256,64]{0,1:T(8,128)(2,1)S(1)} %get-tuple-element.19, bf16[256,64]{0,1:T(8,128)(2,1)S(1)} %get-tuple-element.20), kind=kOutput, calls=%fused_computation.59 | convolution fusion | flops 1082261248 | bytes 21038080 | tf_op jit(solution)/shard_map/sd,pd->sp/dot_general | solution.py:262
  78.6 0.2 fusion.31
  78.9 0.1 convert_reduce_fusion.1
  79.0 3.7 %convert_reduce_fusion = (f32[256]{0:T(256)S(1)}, bf16[256,16384]{1,0:T(8,128)(2,1)S(1)}) fusion(f32[256,16384]{1,0:T(8,128)S(1)} %get-tuple-element.24, f32[256]{0:T(256)S(1)} %max.13), kind=kLoop, calls=%fused_computation.1 | loop fusion | flops 16776960 | bytes 25167872 | tf_op jit(solution)/shard_map/reduce_sum | solution.py:266
  82.7 2.5 %fusion.33 = f32[256,128]{1,0:T(8,128)S(1)} fusion(bf16[256,16384]{1,0:T(8,128)(2,1)S(1)} %get-tuple-element.14, bf16[16384,128]{1,0:T(8,128)(2,1)S(1)} %bitcast.34), kind=kOutput, calls=%fused_computation.60 | convolution fusion | flops 1073741824 | bytes 12713984 | tf_op jit(solution)/shard_map/dot_general | solution.py:267
  85.2 2.8 %fusion.6 = bf16[256,128]{1,0:T(8,128)(2,1)} fusion(f32[256,128]{1,0:T(8,128)S(1)} %fusion.33, bf16[16,256,256]{2,1,0:T(8,128)(2,1)S(1)} %fusion.2, bf16[16,256,128]{2,1,0:T(8,128)(2,1)} %bitcast.40, f32[256]{0:T(256)S(1)} %get-tuple-element.11, f32[256]{0:T(256)S(1)} %get-tuple-element.12, f32[256,256]{0,1:T(8,128)S(1)} %get-tuple-element.22, ...), kind=kOutput, calls=%fused_computation.17 | convolution fusion | flops 285638656 | bytes 3607552 | tf_op jit(solution)/shard_map/dot_general | solution.py:261
  88.0 2.9 %convolution_convert_fusion = bf16[256,4096]{1,0:T(8,128)(2,1)} fusion(bf16[256,128]{1,0:T(8,128)(2,1)} %fusion.6, bf16[128,4096]{1,0:T(8,128)(2,1)S(1)} %copy-done), kind=kOutput, calls=%fused_computation.5 | convolution fusion | flops 269484032 | bytes 3211264 | tf_op jit(solution)/shard_map/dot_general | solution.py:270
  90.9 0.0 reduce-scatter.2.cloned.1.call-update
  91.5 78.6 %reduce-scatter.2.cloned.1.call-done = bf16[16,4096]{1,0:T(8,128)(2,1)} async-done(((bf16[256,4096]{1,0:T(8,128)(2,1)}), bf16[16,4096]{1,0:T(8,128)(2,1)}) %reduce-scatter.2.cloned.1.call-update) | async-done | bytes 131088 | tf_op jit(solution)/shard_map/reduce_scatter | solution.py:212
  170.2 1.6 fusion.8
  (13 shorter events, 0.1 us)
Async XLA Ops:
  6.5 81.4 %copy-start = (bf16[128,4096]{1,0:T(8,128)(2,1)S(1)}, bf16[128,4096]{1,0:T(8,128)(2,1)}, u32[]{:S(2)}) copy-start(bf16[128,4096]{1,0:T(8,128)(2,1)} %param.14) | copy-start | bytes 3145732
  6.5 163.7 %reduce-scatter.2.cloned.1.call-start = ((), (), s32[]{:S(2)}) async-start(), calls=%async_computation.1 | async-start | bytes 2228224 | tf_op jit(solution)/shard_map/reduce_scatter | solution.py:212
  68.6 5.4 %copy-start.3 = (bf16[4096,128]{1,0:T(8,128)(2,1)S(1)}, bf16[4096,128]{1,0:T(8,128)(2,1)}, u32[]{:S(2)}) copy-start(bf16[4096,128]{1,0:T(8,128)(2,1)} %param.12) | copy-start | bytes 3145732
  71.7 3.2 %copy-start.4 = (bf16[4096,128]{1,0:T(8,128)(2,1)S(1)}, bf16[4096,128]{1,0:T(8,128)(2,1)}, u32[]{:S(2)}) copy-start(bf16[4096,128]{1,0:T(8,128)(2,1)} %param.11) | copy-start | bytes 3145732
  74.0 2.2 %copy-start.2 = (bf16[2,4,4,512,128]{4,3,2,1,0:T(8,128)(2,1)S(1)}, bf16[2,4,4,512,128]{4,3,2,1,0:T(8,128)(2,1)}, u32[]{:S(2)}) copy-start(bf16[2,4,4,512,128]{4,3,2,1,0:T(8,128)(2,1)} %get-tuple-element.9) | copy-start | bytes 12582916
  79.0 3.7 %copy-start.1 = (bf16[2,4,4,512,128]{4,3,2,1,0:T(8,128)(2,1)S(1)}, bf16[2,4,4,512,128]{4,3,2,1,0:T(8,128)(2,1)}, u32[]{:S(2)}) copy-start(bf16[2,4,4,512,128]{4,3,2,1,0:T(8,128)(2,1)} %get-tuple-element.10) | copy-start | bytes 12582916
Sparse Core Ops, SparseCore 0:
  91.0 79.1 reduce-scatter.1

commit v2 on v1

--- a/solution.py
+++ b/solution.py
@@ -208,8 +208,108 @@
     )(hidden, prefix_keys, prefix_values)
 
 
+CUT = 4
+
+
+def sum_kernel(p_ref, o_ref, got, made, y_send, y_got, z_s, z_r, y_s, y_r):
+    _, _, _, _, _, z, low = where_am_i()
+    n = neighbours()
+    greet([n["zp"], n["zm"], n["peer"]])
+    half = NZ // 2
+    width = p_ref.shape[-1] // CUT
+    sends = []
+
+    def cols(c):
+        return slice(c * width, (c + 1) * width)
+
+    def starts_at(way, c):
+        return 0 if (c < CUT // 2) == (way == 0) else 1
+
+    def target(way, step):
+        dist = half - step
+        return lax.rem(z + (dist if way == 0 else NZ - dist), NZ)
+
+    def copy(way, step, c, src):
+        return remote(
+            src, got.at[way, step, :, :, cols(c)], z_s.at[way, step, c], z_r.at[way, step, c],
+            n["zp"] if way == 0 else n["zm"],
+        )
+
+    def arrived(way, step, c):
+        copy(way, step, c, got.at[way, step, :, :, cols(c)]).wait_recv()
+        return got[way, step, :, :, cols(c)].astype(jnp.float32)
+
+    def send(way, step, c):
+        first = starts_at(way, c)
+        if step == first:
+            src = p_ref.at[target(way, step), :, :, cols(c)]
+        else:
+            total = arrived(way, step - 1, c) + p_ref[target(way, step), :, :, cols(c)].astype(
+                jnp.float32
+            )
+            made[way, step, :, :, cols(c)] = total.astype(made.dtype)
+            src = made.at[way, step, :, :, cols(c)]
+        one = copy(way, step, c, src)
+        one.start()
+        sends.append(one)
+
+    for step in range(half):
+        order = [(way, c) for c in range(CUT) for way in (0, 1)]
+        for way, c in order:
+            if step >= starts_at(way, c):
+                send(way, step, c)
+
+    def y_copy(c):
+        return remote(
+            y_send.at[:, cols(c)], y_got.at[:, cols(c)], y_s.at[c], y_r.at[c], n["peer"]
+        )
+
+    kept = []
+    for c in range(CUT):
+        for way in (0, 1):
+            copy(way, half - 1, c, got.at[way, half - 1, :, :, cols(c)]).wait_recv()
+
+        def total(side):
+            return (
+                p_ref[z, side, :, cols(c)].astype(jnp.float32)
+                + got[0, half - 1, side, :, cols(c)].astype(jnp.float32)
+                + got[1, half - 1, side, :, cols(c)].astype(jnp.float32)
+            )
+
+        y_send[:, cols(c)] = total(1 - low).astype(y_send.dtype)
+        one = y_copy(c)
+        one.start()
+        sends.append(one)
+        o_ref[:, cols(c)] = total(low)
+    for c in range(CUT):
+        y_copy(c).wait_recv()
+        o_ref[:, cols(c)] += y_got[:, cols(c)].astype(jnp.float32)
+    for one in sends:
+        one.wait_send()
+
+
 def reduce_rows(terms):
-    return lax.psum_scatter(terms, "tp", scatter_dimension=0, tiled=True).astype(jnp.float32)
+    slot, width = terms.shape
+    rows = slot // (NZ * 2)
+    kind = terms.dtype
+    dma = pltpu.SemaphoreType.DMA
+    vmem = pl.BlockSpec(memory_space=pltpu.VMEM)
+    half = NZ // 2
+    return pl.pallas_call(
+        sum_kernel,
+        out_shape=jax.ShapeDtypeStruct((rows, width), jnp.float32),
+        in_specs=[vmem],
+        out_specs=vmem,
+        scratch_shapes=[
+            pltpu.VMEM((2, half, 2, rows, width), kind),
+            pltpu.VMEM((2, half, 2, rows, width), kind),
+            pltpu.VMEM((rows, width), kind),
+            pltpu.VMEM((rows, width), kind),
+            dma((2, half, CUT)), dma((2, half, CUT)), dma((CUT,)), dma((CUT,)),
+        ],
+        compiler_params=pltpu.CompilerParams(collective_id=1, has_side_effects=True),
+        name="sum_heads",
+    )(terms.reshape(NZ, 2, rows, width))
 
 
 def rotate(values, angles):

time: 179 us -> 120 us (0.67)
  waiting for transfers between devices: 78.7 us -> 0 us
  Pallas kernels: 59.8 us -> 92.9 us
  between operations: 14.2 us -> 0.81 us
    reduce_scatter x1 -> x0, waiting for transfers between devices: 78.6 us -> none  [reduce_rows(): lax.psum_scatter(terms, 'tp', scatter_dimension=0, tiled=True)]
    pallas_call x0 -> x1, Pallas kernels: none -> 33.1 us  [reduce_rows(): pl.pallas_call(sum_kernel, out_shape=jax.ShapeDtypeStruct((rows, width),...]
  transfers between devices with their start and end apart: 1 -> 0, of which waited for: 1 -> 0; matrix products, arithmetic and copies ran while one was open for 0% -> 0% of each run, Pallas kernels for 0% -> 0%
where the time goes in v2:
time: 120 us
  Pallas kernels  92.9 us (77%)
  other arithmetic  12.8 us (11%)
  matrix products  12.5 us (10%)
    pallas_call x1, Pallas kernels, gather(): pl.pallas_call(gather_kernel, out_shape=(jax.ShapeDtypeStruct((NZ * 2, *h...  59.8 us
    pallas_call x1, Pallas kernels, reduce_rows(): pl.pallas_call(sum_kernel, out_shape=jax.ShapeDtypeStruct((rows, width),...  33.1 us
    reduce_sum x1, other arithmetic, on_device(): run_total = total * fade + jnp.sum(weights.astype(jnp.float32), axis=-1)  3.78 us
    dot_general x1, matrix products, on_device(): jnp.dot(context, w_out, preferred_element_type=jnp.float32)  2.89 us
    dot_general x1, matrix products, on_device(): acc = jnp.dot(own_weights, value_new, preferred_element_type=jnp.float32)  2.78 us
    dot_general x1, matrix products, on_device(): jnp.einsum('sd,pd->sp', query, keys, preferred_element_type=jnp.float32)  2.47 us

profile of v2, /device:TPU:2, one launch (start us, length us, event | category | flops | bytes accessed | tf_op | source)
XLA Modules:
  0.0 119.8 jit_solution(17848083666071078127)
XLA Ops:
  0.0 0.0 copy-start
  0.0 0.7 broadcast_in_dim.19
  0.8 1.6 %pad_maximum_fusion.h_ref = bf16[272,256]{1,0:T(8,128)(2,1)} fusion(bf16[16,256]{1,0:T(8,128)(2,1)S(1)} %broadcast_in_dim.19, bf16[256,256]{1,0:T(8,128)(2,1)} %bitcast.40), kind=kLoop, calls=%fused_computation.23 | loop fusion | flops 278528 | bytes 278528 | tf_op jit(solution)/shard_map/concatenate | solution.py:330
  2.3 59.8 %gather_all.1 = (bf16[16,272,256]{2,1,0:T(8,128)(2,1)}, bf16[2,4,4,512,128]{4,3,2,1,0:T(8,128)(2,1)}, bf16[2,4,4,512,128]{4,3,2,1,0:T(8,128)(2,1)}) custom-call(bf16[272,256]{1,0:T(8,128)(2,1)} %pad_maximum_fusion.h_ref, bf16[512,128]{1,0:T(8,128)(2,1)} %k_ref.1, bf16[512,128]{1,0:T(8,128)(2,1)} %v_ref.1), custom_call_target="tpu_custom_call" | custom-call | tf_op jit(solution)/shard_map/gather_all/pallas_call | solution.py:197
  62.1 0.0 copy-start.3
  62.1 0.9 slice_convert_fusion
  63.0 2.1 %fusion = f32[256]{0:T(256)S(1)} fusion(bf16[16,272,256]{2,1,0:T(8,128)(2,1)} %get-tuple-element.8), kind=kLoop, calls=%fused_computation.6 | loop fusion | flops 3145472 | bytes 2098176 | tf_op jit(solution)/shard_map/reduce_sum | solution.py:340
  65.2 2.3 %fusion.2 = bf16[16,256,256]{2,1,0:T(8,128)(2,1)S(1)} fusion(f32[16,256]{1,0:T(8,128)S(1)} %bitcast.41, f32[256]{0:T(256)S(1)} %add_rsqrt_fusion, bf16[16,272,256]{2,1,0:T(8,128)(2,1)} %get-tuple-element.8), kind=kLoop, calls=%fused_computation.8 | loop fusion | flops 4194304 | bytes 4211712 | tf_op jit(solution)/shard_map/convert_element_type | solution.py:341
  67.4 0.0 copy-start.2
  67.5 0.0 copy-done.3
  67.5 0.9 convolution_bitcast_fusion.1
  68.3 0.0 copy-done.4
  68.4 0.9 convolution_bitcast_fusion.2
  69.2 0.3 fusion.22
  69.6 0.1 copy-done.2
  69.6 2.5 %fusion.32 = (f32[256]{0:T(256)S(1)}, f32[256,16384]{1,0:T(8,128)S(1)}) fusion(bf16[16384,128]{1,0:T(8,128)(2,1)S(1)} %bitcast.37, bf16[256,64]{0,1:T(8,128)(2,1)S(1)} %get-tuple-element.19, bf16[256,64]{0,1:T(8,128)(2,1)S(1)} %get-tuple-element.20), kind=kOutput, calls=%fused_computation.59 | convolution fusion | flops 1082261248 | bytes 21038080 | tf_op jit(solution)/shard_map/sd,pd->sp/dot_general | solution.py:362
  72.1 0.2 fusion.31
  72.4 3.8 %convert_reduce_fusion = (f32[256]{0:T(256)S(1)}, bf16[256,16384]{1,0:T(8,128)(2,1)S(1)}) fusion(f32[256,16384]{1,0:T(8,128)S(1)} %get-tuple-element.24, f32[256]{0:T(256)S(1)} %max.13), kind=kLoop, calls=%fused_computation.1 | loop fusion | flops 16776960 | bytes 25167872 | tf_op jit(solution)/shard_map/reduce_sum | solution.py:366
  76.2 2.4 %fusion.33 = f32[256,128]{1,0:T(8,128)S(1)} fusion(bf16[256,16384]{1,0:T(8,128)(2,1)S(1)} %get-tuple-element.14, bf16[16384,128]{1,0:T(8,128)(2,1)S(1)} %bitcast.35), kind=kOutput, calls=%fused_computation.60 | convolution fusion | flops 1073741824 | bytes 12713984 | tf_op jit(solution)/shard_map/dot_general | solution.py:367
  78.6 0.1 convert_reduce_fusion.1
  78.6 2.8 %fusion.6 = bf16[256,128]{1,0:T(8,128)(2,1)} fusion(f32[256,128]{1,0:T(8,128)S(1)} %fusion.33, bf16[16,256,256]{2,1,0:T(8,128)(2,1)S(1)} %fusion.2, bf16[16,256,128]{2,1,0:T(8,128)(2,1)} %bitcast.42, f32[256]{0:T(256)S(1)} %get-tuple-element.11, f32[256]{0:T(256)S(1)} %get-tuple-element.12, f32[256,256]{0,1:T(8,128)S(1)} %get-tuple-element.22, ...), kind=kOutput, calls=%fused_computation.17 | convolution fusion | flops 285638656 | bytes 3607552 | tf_op jit(solution)/shard_map/dot_general | solution.py:361
  81.4 2.9 %convolution_convert_fusion = bf16[256,4096]{1,0:T(8,128)(2,1)} fusion(bf16[256,128]{1,0:T(8,128)(2,1)} %fusion.6, bf16[128,4096]{1,0:T(8,128)(2,1)S(1)} %copy-done), kind=kOutput, calls=%fused_computation.5 | convolution fusion | flops 269484032 | bytes 3211264 | tf_op jit(solution)/shard_map/dot_general | solution.py:370
  84.3 33.1 %sum_heads.1 = f32[16,4096]{1,0:T(8,128)} custom-call(bf16[8,2,16,4096]{3,2,1,0:T(8,128)(2,1)} %bitcast.36), custom_call_target="tpu_custom_call" | custom-call | tf_op jit(solution)/shard_map/sum_heads/pallas_call | solution.py:298
  118.1 1.7 %fusion.8 = bf16[1,16,4096]{2,1,0:T(8,128)(2,1)} fusion(f32[16,4096]{1,0:T(8,128)} %sum_heads.1, pred[16]{0:T(512)(128)(4,1)S(1)} %add_compare_fusion), kind=kLoop, calls=%fused_computation.24 | loop fusion | flops 65536 | bytes 393232 | tf_op jit(solution)/shard_map/broadcast_in_dim | solution.py:374
  (11 shorter events, 0.1 us)
Async XLA Ops:
  0.0 81.4 %copy-start = (bf16[128,4096]{1,0:T(8,128)(2,1)S(1)}, bf16[128,4096]{1,0:T(8,128)(2,1)}, u32[]{:S(2)}) copy-start(bf16[128,4096]{1,0:T(8,128)(2,1)} %param.14) | copy-start | bytes 3145732
  62.1 5.4 %copy-start.3 = (bf16[4096,128]{1,0:T(8,128)(2,1)S(1)}, bf16[4096,128]{1,0:T(8,128)(2,1)}, u32[]{:S(2)}) copy-start(bf16[4096,128]{1,0:T(8,128)(2,1)} %param.12) | copy-start | bytes 3145732
  65.1 3.2 %copy-start.4 = (bf16[4096,128]{1,0:T(8,128)(2,1)S(1)}, bf16[4096,128]{1,0:T(8,128)(2,1)}, u32[]{:S(2)}) copy-start(bf16[4096,128]{1,0:T(8,128)(2,1)} %param.11) | copy-start | bytes 3145732
  67.4 2.2 %copy-start.2 = (bf16[2,4,4,512,128]{4,3,2,1,0:T(8,128)(2,1)S(1)}, bf16[2,4,4,512,128]{4,3,2,1,0:T(8,128)(2,1)}, u32[]{:S(2)}) copy-start(bf16[2,4,4,512,128]{4,3,2,1,0:T(8,128)(2,1)} %get-tuple-element.9) | copy-start | bytes 12582916
  72.4 3.8 %copy-start.1 = (bf16[2,4,4,512,128]{4,3,2,1,0:T(8,128)(2,1)S(1)}, bf16[2,4,4,512,128]{4,3,2,1,0:T(8,128)(2,1)}, u32[]{:S(2)}) copy-start(bf16[2,4,4,512,128]{4,3,2,1,0:T(8,128)(2,1)} %get-tuple-element.10) | copy-start | bytes 12582916
